TPU v7x, 32 devices: a whole 2x2x4 slice. The times are simulated.
32 devices in a mesh: comp: 8 (over z, y), harm: 4 (over x, core).
Axes of the slice: x: 2, y: 2, z: 4, core: 2. Of those that a mesh axis runs over, the one named last changes fastest.
Arguments:
- load: float32 [128, 32768], P('harm', 'comp'), may hold values from -6 to 6
- stiff_blocks: bfloat16 [256, 8, 128, 128], P('comp'), as said below
- mass_blocks: bfloat16 [256, 8, 128, 128], P('comp'), as said below
- block_cols: int32 [256, 8], P('comp'), may hold values from -8 to 263, as said below
- contact_rows: int32 [8, 256], P('comp'), may hold values from 0 to 4095, as said below
- partner_slot: int32 [8, 256], P('comp'), may hold values from 0 to 255, each once within a row
- contact_count: int32 [8], P('comp'), may hold values from 32 to 256, as said below
- normal_load: float32 [8, 256], P('comp'), may hold values from 0.3 to 3
- contact_stiffness: float32 [8, 256], P('comp'), may hold values from 0.3 to 3
- frequency: float32 [1], replicated, may hold values from 0.2 to 1
Outputs:
- displacement: float32 [128, 32768], P('harm', 'comp')
- residual: float32 [128, 32768], P('harm', 'comp')
Inputs may be any that keep to these rules, and one draw needn't show every extreme that they name: `block_cols`: entry 0 of block row r is r; its other 7 entries are distinct, differ from r by 1 to 8, and include r - 8 and r + 8; columns outside 0 .. 255 refer to zero parts of the field. `contact_rows`: the 256 entries of one group are distinct. Slots 0 .. contact_count[d]-1 of group d are live; the others carry no force. `stiff_blocks`: slot 0 of every block row is the block on the diagonal. `mass_blocks`: slot 0 of every block row is the block on the diagonal.
All inputs are finite; a program needn't handle non-finite values.
Results may differ from a plain program's by a relative error of at most 0.015.
The roundings to bfloat16 on the way count: a program that leaves them out, or rounds other values in their place, can miss the bound.
Values may be sent and summed in bfloat16 or wider, within the bound.
A program may use at most 64 MiB of HBM per device.

v0:
```python
import functools
import math

import jax
import jax.numpy as jnp
import numpy as np
from jax import lax
from jax.experimental import pallas as pl
from jax.experimental.pallas import tpu as pltpu
from jax.sharding import PartitionSpec as P

H = 128
TIME_POINTS = 1024
BAND = 8
ITERS = 3
MESH = pl.DeviceIdType.MESH
F32 = jnp.float32
BF16 = jnp.bfloat16
NN = (((1,), (0,)), ((), ()))
NT = (((1,), (1,)), ((), ()))


def host_tables(harm_parts):
    column = np.arange(H)
    orders = np.where(column <= H // 2, column, column - H // 2)
    phase = np.arange(TIME_POINTS)[:, None] * orders[None, :] % TIME_POINTS
    angle = phase * (2.0 * math.pi / TIME_POINTS)
    table = np.where(column[None, :] <= H // 2, np.cos(angle), np.sin(angle))
    table = table.astype(np.float32)
    high = table.astype(BF16)
    low = (table - high.astype(np.float32)).astype(BF16)
    to_time = np.concatenate([high, low], axis=1)
    back = np.stack(
        [high.T.reshape(harm_parts, -1, TIME_POINTS), low.T.reshape(harm_parts, -1, TIME_POINTS)], axis=1
    )
    return to_time, back.reshape(harm_parts, -1, TIME_POINTS)


def halves(value):
    high = value.astype(BF16)
    low = (value - high.astype(F32)).astype(BF16)
    return high, low


def stacked(value):
    return jnp.concatenate(halves(value), axis=0)


def folded(value):
    half = value.shape[0] // 2
    return value[:half] + value[half:]


def product(left, right, dims):
    return lax.dot_general(left, right, dims, preferred_element_type=F32)


def kernel(
    comp_size,
    harm_size,
    load_hbm,
    stiff_hbm,
    mass_hbm,
    cols_hbm,
    rows_hbm,
    partner_hbm,
    count_ref,
    normal_hbm,
    spring_hbm,
    freq_ref,
    time_hbm,
    back_hbm,
    disp_out,
    res_out,
    cols_ref,
    rows_ref,
    partner_ref,
    normal_ref,
    spring_ref,
    factor_ref,
    load_ref,
    time_ref,
    back_ref,
    stiff_ref,
    mass_ref,
    field,
    shift,
    dyn_ref,
    inv_ref,
    slot_inverse,
    hot,
    perm,
    ext,
    halo,
    swap_out,
    swap_in,
    shared,
    rel_high,
    rel_low,
    small_sem,
    side_sem,
    diag_sem,
    block_sem,
    halo_send,
    halo_recv,
    swap_send,
    swap_recv,
    share_send,
    share_recv,
):
    comp = lax.axis_index("comp")
    harm = lax.axis_index("harm")
    block_rows = stiff_ref.shape[0]
    slots = stiff_ref.shape[1]
    blk = stiff_ref.shape[2]
    nh = load_ref.shape[0]
    wide = 2 * blk
    pairs = block_rows // 2
    chunks = block_rows // BAND
    cmax = rows_ref.shape[1]
    first_row = comp * block_rows
    has_prev = comp > 0
    has_next = comp < comp_size - 1
    after = lax.rem(comp + 1, comp_size)
    before = lax.rem(comp + comp_size - 1, comp_size)
    facing = lax.rem(comp + comp_size // 2, comp_size)
    order = list(range(1, chunks - 1)) + [0, chunks - 1]

    small_copies = [
        pltpu.make_async_copy(source, held, small_sem.at[i])
        for i, (source, held) in enumerate(
            (
                (rows_hbm, rows_ref),
                (partner_hbm, partner_ref),
                (normal_hbm, normal_ref),
                (spring_hbm, spring_ref),
                (cols_hbm, cols_ref),
            )
        )
    ]
    for copy in small_copies:
        copy.start()
    diag_copies = [
        pltpu.make_async_copy(source.at[:, pl.ds(0, 1)], held.at[:, pl.ds(0, 1)], diag_sem.at[i])
        for i, (source, held) in enumerate(((stiff_hbm, stiff_ref), (mass_hbm, mass_ref)))
    ]
    for copy in diag_copies:
        copy.start()
    load_copy, *table_copies = [
        pltpu.make_async_copy(source, held, side_sem.at[i])
        for i, (source, held) in enumerate(
            ((load_hbm, load_ref), (time_hbm, time_ref), (back_hbm, back_ref))
        )
    ]
    load_copy.start()
    block_copies = {}
    for c in order:
        span = (pl.ds(c * BAND, BAND), pl.ds(1, slots - 1))
        block_copies[c] = [
            pltpu.make_async_copy(source.at[span], held.at[span], block_sem.at[c, i])
            for i, (source, held) in enumerate(((stiff_hbm, stiff_ref), (mass_hbm, mass_ref)))
        ]
        for copy in block_copies[c]:
            copy.start()
    for copy in table_copies:
        copy.start()

    barrier = pltpu.get_barrier_semaphore()
    pl.semaphore_signal(barrier, inc=1, device_id=(facing, harm), device_id_type=MESH)
    for step in range(1, harm_size):
        peer = lax.rem(harm + step, harm_size)
        pl.semaphore_signal(barrier, inc=1, device_id=(comp, peer), device_id_type=MESH)

    @pl.when(has_prev)
    def _():
        pl.semaphore_signal(barrier, inc=1, device_id=(before, harm), device_id_type=MESH)

    @pl.when(has_next)
    def _():
        pl.semaphore_signal(barrier, inc=1, device_id=(after, harm), device_id_type=MESH)

    for copy in small_copies:
        copy.wait()

    row_list = rows_ref[...]
    sub = lax.broadcasted_iota(jnp.int32, (wide, cmax), 0)

    def mark(p, carry):
        base = pl.multiple_of(p * wide, wide)
        hot[pl.ds(base, wide), :] = jnp.where(sub == row_list - base, 1.0, 0.0).astype(BF16)
        return carry

    lax.fori_loop(0, pairs, mark, 0, unroll=2)
    slot_axis = lax.broadcasted_iota(jnp.int32, (cmax, cmax), 0)
    perm[...] = jnp.where(slot_axis == partner_ref[...], 1.0, 0.0).astype(BF16)
    ext[pl.ds(0, BAND)] = jnp.zeros((BAND, nh, blk), BF16)
    ext[pl.ds(BAND + block_rows, BAND)] = jnp.zeros((BAND, nh, blk), BF16)

    def factor_of(width):
        index = harm * nh + lax.broadcasted_iota(jnp.int32, (nh, width), 0)
        wave = jnp.where(index <= H // 2, index, index - H // 2).astype(F32)
        value = freq_ref[0] * wave * (2.0 / H)
        return value * value

    factor_ref[...] = factor_of(wide)
    slot_index = lax.broadcasted_iota(jnp.int32, (1, cmax), 1)
    slot_scale = jnp.where(slot_index < count_ref[0], normal_ref[...], 0.0)
    own_index = harm * nh + lax.broadcasted_iota(jnp.int32, (nh, cmax), 0)
    own_weight = jnp.where(own_index == 0, 1.0 / TIME_POINTS, 2.0 / TIME_POINTS)
    spring_ratio = spring_ref[...] / normal_ref[...]

    for copy in diag_copies:
        copy.wait()
    load_copy.wait()
    eye = lax.broadcasted_iota(jnp.int32, (blk, blk), 0) == lax.broadcasted_iota(
        jnp.int32, (blk, blk), 1
    )

    def diagonal(ref, p):
        parts = [
            jnp.sum(jnp.where(eye, ref[2 * p + q, 0].astype(F32), 0.0), axis=0, keepdims=True)
            for q in range(2)
        ]
        return jnp.concatenate(parts, axis=1)

    def put_rounded(p, value):
        rounded = value.astype(BF16)
        for q in range(2):
            ext[BAND + 2 * p + q] = rounded[:, q * blk : (q + 1) * blk]

    def lanes(p):
        return pl.ds(pl.multiple_of(p * wide, wide), wide)

    def start_field(p, gathered):
        stiff_diag = diagonal(stiff_ref, p)
        mass_diag = diagonal(mass_ref, p)
        dynamic = stiff_diag - factor_ref[...] * mass_diag
        inverse = 1.0 / dynamic
        value = load_ref[:, lanes(p)] * inverse
        dyn_ref[p] = dynamic
        inv_ref[p] = inverse
        field[p] = value
        put_rounded(p, value)
        high, low = halves(value)
        diagonals = jnp.concatenate(
            [jnp.broadcast_to(part, (8, wide)) for part in (stiff_diag, mass_diag)], axis=0
        )
        left = jnp.concatenate([high, low, diagonals.astype(BF16)], axis=0)
        return gathered + product(left, hot[lanes(p), :], NN)

    gathered = lax.fori_loop(
        0, pairs, start_field, jnp.zeros((2 * nh + 16, cmax), F32), unroll=4
    )
    listed = folded(gathered[: 2 * nh])
    slot_dynamic = gathered[2 * nh : 2 * nh + 1] - factor_of(cmax) * gathered[2 * nh + 8 : 2 * nh + 9]
    slot_inverse[...] = 1.0 / slot_dynamic

    neighbours = jnp.minimum(comp, 1) + jnp.minimum(comp_size - 1 - comp, 1)
    pl.semaphore_wait(barrier, harm_size + neighbours)

    def apply_rows(first, stop, gathered):
        def body(p, carry):
            applied = []
            for q in range(2):
                r = 2 * p + q
                picked = jnp.concatenate(
                    [
                        ext[jnp.clip(cols_ref[s, r] - first_row + BAND, 0, ext.shape[0] - 1)]
                        for s in range(slots)
                    ],
                    axis=1,
                )
                blocks = jnp.concatenate(
                    [
                        jnp.concatenate([ref[r, s] for s in range(slots)], axis=1)
                        for ref in (stiff_ref, mass_ref)
                    ],
                    axis=0,
                )
                both = product(picked, blocks, NT)
                applied.append(both[:, :blk] - factor_ref[:, :blk] * both[:, blk:])
            rounded = jnp.concatenate([ext[BAND + 2 * p + q] for q in range(2)], axis=1)
            gap = field[p] - rounded.astype(F32)
            value = load_ref[:, lanes(p)] - jnp.concatenate(applied, axis=1) - dyn_ref[p] * gap
            shift[p] = value
            if carry is None:
                return carry
            return carry + product(stacked(value), hot[lanes(p), :], NN)

        return lax.fori_loop(first * BAND // 2, stop * BAND // 2, body, gathered, unroll=4)

    def swap_copy(k):
        return pltpu.make_async_remote_copy(
            src_ref=swap_out.at[k],
            dst_ref=swap_in.at[k],
            send_sem=swap_send.at[k],
            recv_sem=swap_recv.at[k],
            device_id=(facing, harm),
            device_id_type=MESH,
        )

    def halo_copies(k):
        up = pltpu.make_async_remote_copy(
            src_ref=ext.at[pl.ds(block_rows, BAND)],
            dst_ref=halo.at[k, 0],
            send_sem=halo_send.at[k, 0],
            recv_sem=halo_recv.at[k, 0],
            device_id=(after, harm),
            device_id_type=MESH,
        )
        down = pltpu.make_async_remote_copy(
            src_ref=ext.at[pl.ds(BAND, BAND)],
            dst_ref=halo.at[k, 1],
            send_sem=halo_send.at[k, 1],
            recv_sem=halo_recv.at[k, 1],
            device_id=(before, harm),
            device_id_type=MESH,
        )
        return up, down

    def start_halo(k):
        up, down = halo_copies(k)

        @pl.when(has_next)
        def _():
            up.start()

        @pl.when(has_prev)
        def _():
            down.start()

    swap_out[0] = listed
    swap_copy(0).start()
    start_halo(0)

    for k in range(ITERS):
        up, down = halo_copies(k)
        last = k == ITERS - 1

        def span(first, stop, gathered):
            if k > 0:
                return apply_rows(first, stop, gathered)
            for chunk in range(first, stop):
                for copy in block_copies[chunk]:
                    copy.wait()
                gathered = apply_rows(chunk, chunk + 1, gathered)
            return gathered

        gathered = None if last else jnp.zeros((2 * nh, cmax), F32)
        gathered = span(1, chunks - 1, gathered)

        swap_copy(k).wait()
        mirrored = folded(product(stacked(swap_in[k]), perm[...], NN))
        shared[k, harm] = (swap_out[k] - mirrored) * spring_ratio
        sends = []
        for step in range(1, harm_size):
            sends.append(
                pltpu.make_async_remote_copy(
                    src_ref=shared.at[k, harm],
                    dst_ref=shared.at[k, harm],
                    send_sem=share_send.at[k, step - 1],
                    recv_sem=share_recv.at[k, step - 1],
                    device_id=(comp, lax.rem(harm + step, harm_size)),
                    device_id_type=MESH,
                )
            )
            sends[-1].start()

        @pl.when(has_next)
        def _():
            up.wait_send()
            down.wait_recv()
            ext[pl.ds(BAND + block_rows, BAND)] = halo[k, 1]

        @pl.when(has_prev)
        def _():
            down.wait_send()
            up.wait_recv()
            ext[pl.ds(0, BAND)] = halo[k, 0]

        gathered = span(0, 1, gathered)
        gathered = span(chunks - 1, chunks, gathered)

        if k == 0:
            for copy in table_copies:
                copy.wait()
        for send in sends:
            send.wait()
        for part in range(harm_size):
            high, low = halves(shared[k, part])
            for copy in range(2):
                rel_high[pl.ds(copy * H + part * nh, nh), :] = high
                rel_low[pl.ds(copy * H + part * nh, nh), :] = low
        total = jnp.zeros((2 * nh, cmax), F32)
        extra = jnp.zeros((nh, cmax), F32)
        step_points = 2 * H
        for t in range(0, TIME_POINTS, step_points):
            rows_now = time_ref[pl.ds(t, step_points), :]
            values = product(rows_now, rel_high[...], NN) + product(rows_now, rel_low[...], NN)
            high, low = halves(jnp.tanh(values))
            back = back_ref[harm, :, pl.ds(t, step_points)]
            total = total + product(back, high, NN)
            extra = extra + product(back[:nh], low, NN)
        force = (folded(total) + extra) * own_weight * slot_scale
        projected = stacked(force)
        if not last:
            swap_out[k + 1] = swap_out[k] + (folded(gathered) - force) * slot_inverse[...]
            swap_copy(k + 1).start()

        def finish(p, carry):
            nonlinear = folded(product(projected, hot[lanes(p), :], NT))
            residual = shift[p] - nonlinear
            value = field[p] + residual * inv_ref[p]
            if last:
                disp_out[:, lanes(p)] = value
                res_out[:, lanes(p)] = residual
            else:
                field[p] = value
                put_rounded(p, value)
            return carry

        edge = BAND // 2
        lax.fori_loop(0, edge, finish, 0, unroll=edge)
        lax.fori_loop(pairs - edge, pairs, finish, 0, unroll=edge)
        if not last:
            start_halo(k + 1)
        lax.fori_loop(edge, pairs - edge, finish, 0, unroll=8)


def local(comp_size, harm_size, *arrays):
    load, stiff_blocks, mass_blocks, block_cols = arrays[:4]
    nh, dofs = load.shape
    block_rows, slots, blk, _ = stiff_blocks.shape
    cmax = arrays[4].shape[1]
    to_time, back = host_tables(harm_size)
    vmem = pl.BlockSpec(memory_space=pltpu.VMEM)
    smem = pl.BlockSpec(memory_space=pltpu.SMEM)
    hbm = pl.BlockSpec(memory_space=pltpu.HBM)
    wide = (block_rows // 2, nh, 2 * blk)
    dma = pltpu.SemaphoreType.DMA
    return pl.pallas_call(
        functools.partial(kernel, comp_size, harm_size),
        out_shape=(jax.ShapeDtypeStruct((nh, dofs), F32),) * 2,
        in_specs=[hbm, hbm, hbm, hbm, hbm, hbm, smem, hbm, hbm, smem, hbm, hbm],
        out_specs=(vmem, vmem),
        scratch_shapes=[
            pltpu.SMEM((slots, block_rows), jnp.int32),
            pltpu.VMEM((1, cmax), jnp.int32),
            pltpu.VMEM((1, cmax), jnp.int32),
            pltpu.VMEM((1, cmax), F32),
            pltpu.VMEM((1, cmax), F32),
            pltpu.VMEM((nh, 2 * blk), F32),
            pltpu.VMEM(load.shape, F32),
            pltpu.VMEM(to_time.shape, BF16),
            pltpu.VMEM(back.shape, BF16),
            pltpu.VMEM(stiff_blocks.shape, BF16),
            pltpu.VMEM(mass_blocks.shape, BF16),
            pltpu.VMEM(wide, F32),
            pltpu.VMEM(wide, F32),
            pltpu.VMEM(wide, F32),
            pltpu.VMEM(wide, F32),
            pltpu.VMEM((nh, cmax), F32),
            pltpu.VMEM((dofs, cmax), BF16),
            pltpu.VMEM((cmax, cmax), BF16),
            pltpu.VMEM((block_rows + 2 * BAND, nh, blk), BF16),
            pltpu.VMEM((ITERS, 2, BAND, nh, blk), BF16),
            pltpu.VMEM((ITERS, nh, cmax), F32),
            pltpu.VMEM((ITERS, nh, cmax), F32),
            pltpu.VMEM((ITERS, harm_size, nh, cmax), F32),
            pltpu.VMEM((2 * H, cmax), BF16),
            pltpu.VMEM((2 * H, cmax), BF16),
            dma((5,)),
            dma((3,)),
            dma((2,)),
            dma((block_rows // BAND, 2)),
            dma((ITERS, 2)),
            dma((ITERS, 2)),
            dma((ITERS,)),
            dma((ITERS,)),
            dma((ITERS, harm_size - 1)),
            dma((ITERS, harm_size - 1)),
        ],
        compiler_params=pltpu.CompilerParams(
            collective_id=0, has_side_effects=True, vmem_limit_bytes=52 * 1024 * 1024
        ),
    )(load, stiff_blocks, mass_blocks, block_cols.T, *arrays[4:], jnp.asarray(to_time), jnp.asarray(back))


def solution(mesh):
    placed = (
        P("harm", "comp"),
        P("comp", None, None, None),
        P("comp", None, None, None),
        P("comp", None),
        P("comp", None),
        P("comp", None),
        P("comp"),
        P("comp", None),
        P("comp", None),
        P(),
    )
    return jax.shard_map(
        functools.partial(local, mesh.shape["comp"], mesh.shape["harm"]),
        mesh=mesh,
        in_specs=placed,
        out_specs=(P("harm", "comp"), P("harm", "comp")),
        check_vma=False,
    )
```

profile of v0, /device:TPU:0, one launch (start us, length us, event | category | flops | bytes accessed | tf_op | source)
XLA Modules:
  0.0 40.6 jit_solution(7610599008430736598)
XLA Ops:
  1.9 0.0 copy-start
  1.9 1.0 %copy-done = f32[32,4096]{1,0:T(8,128)S(1)} copy-done((f32[32,4096]{1,0:T(8,128)S(1)}, f32[32,4096]{1,0:T(8,128)}, u32[]{:S(2)}) %copy-start) | copy-done | bytes 524312
  3.0 0.0 copy-start.1
  3.0 0.7 %copy-done.1 = s32[32,8]{0,1:T(8,128)S(1)} copy-done((s32[32,8]{0,1:T(8,128)S(1)}, s32[32,8]{0,1:T(8,128)}, u32[]{:S(2)}) %copy-start.1) | copy-done | bytes 1048
  3.7 0.0 copy-start.2
  3.7 0.7 %copy-done.2 = s32[1,256]{1,0:T(1,128)S(1)} copy-done((s32[1,256]{1,0:T(1,128)S(1)}, s32[1,256]{1,0:T(1,128)}, u32[]{:S(2)}) %copy-start.2) | copy-done | bytes 1048
  4.3 0.0 copy-start.3
  4.3 0.7 %copy-done.3 = s32[1,256]{1,0:T(1,128)S(1)} copy-done((s32[1,256]{1,0:T(1,128)S(1)}, s32[1,256]{1,0:T(1,128)}, u32[]{:S(2)}) %copy-start.3) | copy-done | bytes 1048
  5.0 0.0 copy-start.4
  5.0 0.7 %copy-done.4 = f32[1,256]{1,0:T(1,128)S(1)} copy-done((f32[1,256]{1,0:T(1,128)S(1)}, f32[1,256]{1,0:T(1,128)}, u32[]{:S(2)}) %copy-start.4) | copy-done | bytes 1048
  5.7 0.0 copy-start.5
  5.7 0.7 %copy-done.5 = f32[1,256]{1,0:T(1,128)S(1)} copy-done((f32[1,256]{1,0:T(1,128)S(1)}, f32[1,256]{1,0:T(1,128)}, u32[]{:S(2)}) %copy-start.5) | copy-done | bytes 1048
  6.4 32.7 %shard_map.131 = (f32[32,4096]{1,0:T(8,128)S(1)}, f32[32,4096]{1,0:T(8,128)S(1)}) custom-call(f32[32,4096]{1,0:T(8,128)S(1)} %copy-done, bf16[32,8,128,128]{3,2,1,0:T(8,128)(2,1)} %stiff_hbm.1, bf16[32,8,128,128]{3,2,1,0:T(8,128)(2,1)} %mass_hbm.1, s32[8,32]{1,0:T(8,128)S(1)} %bitcast.1, s32[1,256]{1,0:T(1,128)S(1)} %copy-done.2, s32[1,256]{1,0:T(1,128)S(1)} %copy-done.3, ...), custom_call_target="tpu_custom_call" | custom-call | tf_op jit(solution)/shard_map/pallas_call | solution.py:441
  39.1 0.8 %copy.18 = f32[32,4096]{1,0:T(8,128)} copy(f32[32,4096]{1,0:T(8,128)S(1)} %get-tuple-element.4) | data formatting | bytes 1048576
  39.8 0.8 %copy.19 = f32[32,4096]{1,0:T(8,128)} copy(f32[32,4096]{1,0:T(8,128)S(1)} %get-tuple-element.5) | data formatting | bytes 1048576
Async XLA Ops:
  1.9 1.0 %copy-start = (f32[32,4096]{1,0:T(8,128)S(1)}, f32[32,4096]{1,0:T(8,128)}, u32[]{:S(2)}) copy-start(f32[32,4096]{1,0:T(8,128)} %load_hbm.1) | copy-start | bytes 1572868
  3.0 0.7 %copy-start.1 = (s32[32,8]{0,1:T(8,128)S(1)}, s32[32,8]{0,1:T(8,128)}, u32[]{:S(2)}) copy-start(s32[32,8]{0,1:T(8,128)} %param.15) | copy-start | bytes 3076
  3.7 0.7 %copy-start.2 = (s32[1,256]{1,0:T(1,128)S(1)}, s32[1,256]{1,0:T(1,128)}, u32[]{:S(2)}) copy-start(s32[1,256]{1,0:T(1,128)} %rows_hbm.1) | copy-start | bytes 3076
  4.3 0.7 %copy-start.3 = (s32[1,256]{1,0:T(1,128)S(1)}, s32[1,256]{1,0:T(1,128)}, u32[]{:S(2)}) copy-start(s32[1,256]{1,0:T(1,128)} %partner_hbm.1) | copy-start | bytes 3076
  5.0 0.7 %copy-start.4 = (f32[1,256]{1,0:T(1,128)S(1)}, f32[1,256]{1,0:T(1,128)}, u32[]{:S(2)}) copy-start(f32[1,256]{1,0:T(1,128)} %normal_hbm.1) | copy-start | bytes 3076
  5.7 0.7 %copy-start.5 = (f32[1,256]{1,0:T(1,128)S(1)}, f32[1,256]{1,0:T(1,128)}, u32[]{:S(2)}) copy-start(f32[1,256]{1,0:T(1,128)} %spring_hbm.1) | copy-start | bytes 3076
where the time goes:
time: 40.9 us; the launch traced here: 40.6 us
  Pallas kernels  32.7 us (80%)
  local copies, waits for them, and re-layouts  6.02 us (15%)
  between operations  1.95 us (5%)
    pallas_call x1, Pallas kernels, local(): pl.pallas_call(functools.partial(kernel, comp_size, harm_size), out_shape...  32.7 us
    unnamed x14, local copies, waits for them, and re-layouts  6.02 us

commit v1 on v0

--- a/solution.py
+++ b/solution.py
@@ -29,7 +29,7 @@
     table = table.astype(np.float32)
     high = table.astype(BF16)
     low = (table - high.astype(np.float32)).astype(BF16)
-    to_time = np.concatenate([high, low], axis=1)
+    to_time = np.concatenate([high, high], axis=1)
     back = np.stack(
         [high.T.reshape(harm_parts, -1, TIME_POINTS), low.T.reshape(harm_parts, -1, TIME_POINTS)], axis=1
     )
@@ -92,19 +92,17 @@
     perm,
     ext,
     halo,
-    swap_out,
-    swap_in,
+    listed_ref,
+    sent_ref,
     shared,
-    rel_high,
-    rel_low,
+    relative_ref,
+    rel_parts,
     small_sem,
     side_sem,
     diag_sem,
     block_sem,
     halo_send,
     halo_recv,
-    swap_send,
-    swap_recv,
     share_send,
     share_recv,
 ):
@@ -166,10 +164,10 @@
         copy.start()
 
     barrier = pltpu.get_barrier_semaphore()
-    pl.semaphore_signal(barrier, inc=1, device_id=(facing, harm), device_id_type=MESH)
-    for step in range(1, harm_size):
-        peer = lax.rem(harm + step, harm_size)
-        pl.semaphore_signal(barrier, inc=1, device_id=(comp, peer), device_id_type=MESH)
+    partners = [(comp, lax.rem(harm + step, harm_size)) for step in range(1, harm_size)]
+    partners += [(facing, lax.rem(harm + step, harm_size)) for step in range(harm_size)]
+    for partner in partners:
+        pl.semaphore_signal(barrier, inc=1, device_id=partner, device_id_type=MESH)
 
     @pl.when(has_prev)
     def _():
@@ -256,7 +254,7 @@
     slot_inverse[...] = 1.0 / slot_dynamic
 
     neighbours = jnp.minimum(comp, 1) + jnp.minimum(comp_size - 1 - comp, 1)
-    pl.semaphore_wait(barrier, harm_size + neighbours)
+    pl.semaphore_wait(barrier, len(partners) + neighbours)
 
     def apply_rows(first, stop, gathered):
         def body(p, carry):
@@ -289,15 +287,30 @@
 
         return lax.fori_loop(first * BAND // 2, stop * BAND // 2, body, gathered, unroll=4)
 
-    def swap_copy(k):
-        return pltpu.make_async_remote_copy(
-            src_ref=swap_out.at[k],
-            dst_ref=swap_in.at[k],
-            send_sem=swap_send.at[k],
-            recv_sem=swap_recv.at[k],
-            device_id=(facing, harm),
-            device_id_type=MESH,
-        )
+    own = pl.ds(pl.multiple_of(harm * nh, nh), nh)
+
+    def share_copies(k):
+        return [
+            pltpu.make_async_remote_copy(
+                src_ref=shared.at[k, 0, own],
+                dst_ref=shared.at[k, 0 if i < harm_size - 1 else 1, own],
+                send_sem=share_send.at[k, i],
+                recv_sem=share_recv.at[k, i],
+                device_id=partner,
+                device_id_type=MESH,
+            )
+            for i, partner in enumerate(partners)
+        ]
+
+    def share(k, listed):
+        listed_ref[...] = listed
+        change = listed if k == 0 else listed - sent_ref[...]
+        rounded = change.astype(BF16)
+        shared[k, 0, own] = rounded
+        for copy in share_copies(k):
+            copy.start()
+        sent = rounded.astype(F32)
+        sent_ref[...] = sent if k == 0 else sent_ref[...] + sent
 
     def halo_copies(k):
         up = pltpu.make_async_remote_copy(
@@ -329,8 +342,7 @@
         def _():
             down.start()
 
-    swap_out[0] = listed
-    swap_copy(0).start()
+    share(0, listed)
     start_halo(0)
 
     for k in range(ITERS):
@@ -349,23 +361,6 @@
         gathered = None if last else jnp.zeros((2 * nh, cmax), F32)
         gathered = span(1, chunks - 1, gathered)
 
-        swap_copy(k).wait()
-        mirrored = folded(product(stacked(swap_in[k]), perm[...], NN))
-        shared[k, harm] = (swap_out[k] - mirrored) * spring_ratio
-        sends = []
-        for step in range(1, harm_size):
-            sends.append(
-                pltpu.make_async_remote_copy(
-                    src_ref=shared.at[k, harm],
-                    dst_ref=shared.at[k, harm],
-                    send_sem=share_send.at[k, step - 1],
-                    recv_sem=share_recv.at[k, step - 1],
-                    device_id=(comp, lax.rem(harm + step, harm_size)),
-                    device_id_type=MESH,
-                )
-            )
-            sends[-1].start()
-
         @pl.when(has_next)
         def _():
             up.wait_send()
@@ -384,28 +379,22 @@
         if k == 0:
             for copy in table_copies:
                 copy.wait()
-        for send in sends:
-            send.wait()
-        for part in range(harm_size):
-            high, low = halves(shared[k, part])
-            for copy in range(2):
-                rel_high[pl.ds(copy * H + part * nh, nh), :] = high
-                rel_low[pl.ds(copy * H + part * nh, nh), :] = low
+        for copy in share_copies(k):
+            copy.wait()
+        change = shared[k, 0].astype(F32) - product(shared[k, 1], perm[...], NN)
+        relative = change if k == 0 else relative_ref[...] + change
+        relative_ref[...] = relative
+        rel_parts[...] = stacked(relative * spring_ratio)
         total = jnp.zeros((2 * nh, cmax), F32)
-        extra = jnp.zeros((nh, cmax), F32)
         step_points = 2 * H
         for t in range(0, TIME_POINTS, step_points):
-            rows_now = time_ref[pl.ds(t, step_points), :]
-            values = product(rows_now, rel_high[...], NN) + product(rows_now, rel_low[...], NN)
-            high, low = halves(jnp.tanh(values))
-            back = back_ref[harm, :, pl.ds(t, step_points)]
-            total = total + product(back, high, NN)
-            extra = extra + product(back[:nh], low, NN)
-        force = (folded(total) + extra) * own_weight * slot_scale
+            values = product(time_ref[pl.ds(t, step_points), :], rel_parts[...], NN)
+            wave = jnp.tanh(values).astype(BF16)
+            total = total + product(back_ref[harm, :, pl.ds(t, step_points)], wave, NN)
+        force = folded(total) * own_weight * slot_scale
         projected = stacked(force)
         if not last:
-            swap_out[k + 1] = swap_out[k] + (folded(gathered) - force) * slot_inverse[...]
-            swap_copy(k + 1).start()
+            share(k + 1, listed_ref[...] + (folded(gathered) - force) * slot_inverse[...])
 
         def finish(p, carry):
             nonlinear = folded(product(projected, hot[lanes(p), :], NT))
@@ -438,10 +427,12 @@
     hbm = pl.BlockSpec(memory_space=pltpu.HBM)
     wide = (block_rows // 2, nh, 2 * blk)
     dma = pltpu.SemaphoreType.DMA
+    places = [hbm, hbm, hbm, hbm, hbm, hbm, smem, hbm, hbm, smem, hbm, hbm]
+    operands = (load, stiff_blocks, mass_blocks, block_cols.T, *arrays[4:], jnp.asarray(to_time), jnp.asarray(back))
     return pl.pallas_call(
         functools.partial(kernel, comp_size, harm_size),
         out_shape=(jax.ShapeDtypeStruct((nh, dofs), F32),) * 2,
-        in_specs=[hbm, hbm, hbm, hbm, hbm, hbm, smem, hbm, hbm, smem, hbm, hbm],
+        in_specs=places,
         out_specs=(vmem, vmem),
         scratch_shapes=[
             pltpu.SMEM((slots, block_rows), jnp.int32),
@@ -464,10 +455,10 @@
             pltpu.VMEM((cmax, cmax), BF16),
             pltpu.VMEM((block_rows + 2 * BAND, nh, blk), BF16),
             pltpu.VMEM((ITERS, 2, BAND, nh, blk), BF16),
-            pltpu.VMEM((ITERS, nh, cmax), F32),
-            pltpu.VMEM((ITERS, nh, cmax), F32),
-            pltpu.VMEM((ITERS, harm_size, nh, cmax), F32),
-            pltpu.VMEM((2 * H, cmax), BF16),
+            pltpu.VMEM((nh, cmax), F32),
+            pltpu.VMEM((nh, cmax), F32),
+            pltpu.VMEM((ITERS, 2, H, cmax), BF16),
+            pltpu.VMEM((H, cmax), F32),
             pltpu.VMEM((2 * H, cmax), BF16),
             dma((5,)),
             dma((3,)),
@@ -475,15 +466,18 @@
             dma((block_rows // BAND, 2)),
             dma((ITERS, 2)),
             dma((ITERS, 2)),
-            dma((ITERS,)),
-            dma((ITERS,)),
-            dma((ITERS, harm_size - 1)),
-            dma((ITERS, harm_size - 1)),
+            dma((ITERS, 2 * harm_size - 1)),
+            dma((ITERS, 2 * harm_size - 1)),
         ],
         compiler_params=pltpu.CompilerParams(
             collective_id=0, has_side_effects=True, vmem_limit_bytes=52 * 1024 * 1024
         ),
-    )(load, stiff_blocks, mass_blocks, block_cols.T, *arrays[4:], jnp.asarray(to_time), jnp.asarray(back))
+    )(
+        *(
+            pltpu.with_memory_space_constraint(value, pltpu.HBM) if where is hbm else value
+            for value, where in zip(operands, places)
+        )
+    )
 
 
 def solution(mesh):

time: 40.9 us -> 40 us (0.978)
  local copies, waits for them, and re-layouts: 6.02 us -> 1.59 us
  Pallas kernels: 32.7 us -> 36.1 us
    unnamed x14 -> x2, local copies, waits for them, and re-layouts: 6.02 us -> 1.59 us
    pallas_call x1, Pallas kernels: 32.7 us -> 36.1 us  [local(): pl.pallas_call(functools.partial(kernel, comp_size, harm_size), out_shape...]
where the time goes in v1:
time: 40 us; the launch traced here: 39.6 us
  Pallas kernels  36.1 us (90%)
  between operations  1.93 us (5%)
  local copies, waits for them, and re-layouts  1.59 us (4%)
    pallas_call x1, Pallas kernels, local(): pl.pallas_call(functools.partial(kernel, comp_size, harm_size), out_shape...  36.1 us
    unnamed x2, local copies, waits for them, and re-layouts  1.59 us

profile of v1, /device:TPU:0, one launch (start us, length us, event | category | flops | bytes accessed | tf_op | source)
XLA Modules:
  0.0 39.6 jit_solution(13718348860511518328)
XLA Ops:
  1.9 36.1 %shard_map.131 = (f32[32,4096]{1,0:T(8,128)S(1)}, f32[32,4096]{1,0:T(8,128)S(1)}) custom-call(f32[32,4096]{1,0:T(8,128)} %load_hbm.1, bf16[32,8,128,128]{3,2,1,0:T(8,128)(2,1)} %stiff_hbm.1, bf16[32,8,128,128]{3,2,1,0:T(8,128)(2,1)} %mass_hbm.1, s32[8,32]{1,0:T(8,128)} %bitcast.1, s32[1,256]{1,0:T(1,128)} %rows_hbm.1, s32[1,256]{1,0:T(1,128)} %partner_hbm.1, ...), custom_call_target="tpu_custom_call" | custom-call | tf_op jit(solution)/shard_map/pallas_call | solution.py:432
  38.0 0.8 %copy.18 = f32[32,4096]{1,0:T(8,128)} copy(f32[32,4096]{1,0:T(8,128)S(1)} %get-tuple-element.4) | data formatting | bytes 1048576
  38.8 0.8 %copy.19 = f32[32,4096]{1,0:T(8,128)} copy(f32[32,4096]{1,0:T(8,128)S(1)} %get-tuple-element.5) | data formatting | bytes 1048576

commit v2 on v1

v2 whole, which is shorter than its diff:
```python
import functools
import math

import jax
import jax.numpy as jnp
import numpy as np
from jax import lax
from jax.experimental import pallas as pl
from jax.experimental.pallas import tpu as pltpu
from jax.sharding import PartitionSpec as P

H = 128
TIME_POINTS = 1024
BAND = 8
ITERS = 3
MESH = pl.DeviceIdType.MESH
F32 = jnp.float32
BF16 = jnp.bfloat16
NN = (((1,), (0,)), ((), ()))
NT = (((1,), (1,)), ((), ()))


def host_tables(pair_parts):
    column = np.arange(H)
    orders = np.where(column <= H // 2, column, column - H // 2)
    phase = np.arange(TIME_POINTS)[:, None] * orders[None, :] % TIME_POINTS
    angle = phase * (2.0 * math.pi / TIME_POINTS)
    table = np.where(column[None, :] <= H // 2, np.cos(angle), np.sin(angle))
    table = table.astype(np.float32)
    high = table.astype(BF16)
    low = (table - high.astype(np.float32)).astype(BF16)
    to_time = np.concatenate([high, high], axis=1)
    back = np.stack(
        [high.T.reshape(pair_parts, -1, TIME_POINTS), low.T.reshape(pair_parts, -1, TIME_POINTS)], axis=1
    )
    return to_time, back.reshape(pair_parts, -1, TIME_POINTS)


def halves(value):
    high = value.astype(BF16)
    low = (value - high.astype(F32)).astype(BF16)
    return high, low


def stacked(value):
    return jnp.concatenate(halves(value), axis=0)


def folded(value):
    half = value.shape[0] // 2
    return value[:half] + value[half:]


def product(left, right, dims):
    return lax.dot_general(left, right, dims, preferred_element_type=F32)


def kernel(
    comp_size,
    harm_size,
    load_hbm,
    stiff_hbm,
    mass_hbm,
    cols_hbm,
    rows_hbm,
    partner_hbm,
    count_ref,
    normal_hbm,
    spring_hbm,
    freq_ref,
    time_hbm,
    back_hbm,
    disp_out,
    res_out,
    cols_ref,
    rows_ref,
    partner_ref,
    normal_ref,
    spring_ref,
    factor_ref,
    load_ref,
    time_ref,
    back_ref,
    stiff_ref,
    mass_ref,
    field,
    shift,
    dyn_ref,
    inv_ref,
    slot_inverse,
    hot,
    perm,
    ext,
    halo,
    part_ref,
    mate_part,
    listed_ref,
    sent_ref,
    shared,
    relative_ref,
    rel_parts,
    out_stage,
    small_sem,
    side_sem,
    diag_sem,
    block_sem,
    load_sem,
    halo_send,
    halo_recv,
    part_send,
    part_recv,
    share_send,
    share_recv,
    out_send,
    out_recv,
):
    comp = lax.axis_index("comp")
    harm = lax.axis_index("harm")
    core = lax.rem(harm, 2)
    mate = harm + 1 - 2 * core
    block_rows = stiff_ref.shape[0]
    slots = stiff_ref.shape[1]
    blk = stiff_ref.shape[2]
    both_nh = load_ref.shape[0]
    nh = both_nh // 2
    half = block_rows * blk
    wide = 2 * blk
    pairs = block_rows // 2
    chunks = block_rows // BAND
    span = BAND // 2
    cmax = rows_ref.shape[1]
    row0 = core * block_rows
    first_row = comp * 2 * block_rows + row0
    outer = comp + 2 * core - 1
    has_outer = jnp.logical_and(outer >= 0, outer < comp_size)
    outer = lax.rem(outer + comp_size, comp_size)
    facing = lax.rem(comp + comp_size // 2, comp_size)
    outside = core * (chunks - 1)
    inside = (1 - core) * (chunks - 1)
    middle = list(range(1, chunks - 1))
    order = [inside, *middle, outside]
    first_side = 0
    last_side = BAND + block_rows
    outside_halo = core * last_side
    inside_halo = (1 - core) * last_side

    small_copies = [
        pltpu.make_async_copy(source, held, small_sem.at[i])
        for i, (source, held) in enumerate(
            (
                (rows_hbm, rows_ref),
                (partner_hbm, partner_ref),
                (normal_hbm, normal_ref),
                (spring_hbm, spring_ref),
                (cols_hbm, cols_ref),
            )
        )
    ]
    for copy in small_copies:
        copy.start()
    own_rows = pl.ds(pl.multiple_of(core * nh, nh), nh)
    own_half = pl.ds(pl.multiple_of(core * half, half), half)
    mate_half = pl.ds(pl.multiple_of((1 - core) * half, half), half)
    here = pl.ds(row0, block_rows)
    diag_copies = [
        pltpu.make_async_copy(source.at[here, pl.ds(0, 1)], held.at[:, pl.ds(0, 1)], diag_sem.at[i])
        for i, (source, held) in enumerate(((stiff_hbm, stiff_ref), (mass_hbm, mass_ref)))
    ]
    for copy in diag_copies:
        copy.start()
    load_copy, *table_copies = [
        pltpu.make_async_copy(source, held, side_sem.at[i])
        for i, (source, held) in enumerate(
            (
                (load_hbm.at[:, own_half], load_ref.at[own_rows]),
                (time_hbm, time_ref),
                (back_hbm.at[harm // 2], back_ref),
            )
        )
    ]
    load_copy.start()
    block_copies = []
    for n, c in enumerate(order):
        source_span = (pl.ds(row0 + c * BAND, BAND), pl.ds(1, slots - 1))
        held_span = (pl.ds(c * BAND, BAND), pl.ds(1, slots - 1))
        block_copies.append(
            [
                pltpu.make_async_copy(source.at[source_span], held.at[held_span], block_sem.at[n, i])
                for i, (source, held) in enumerate(((stiff_hbm, stiff_ref), (mass_hbm, mass_ref)))
            ]
        )

    barrier = pltpu.get_barrier_semaphore()
    partners = [(comp, lax.rem(harm + step, harm_size)) for step in range(1, harm_size)]
    partners += [(facing, lax.rem(harm + step, harm_size)) for step in range(harm_size)]
    for partner in partners:
        pl.semaphore_signal(barrier, inc=1, device_id=partner, device_id_type=MESH)

    @pl.when(has_outer)
    def _():
        pl.semaphore_signal(barrier, inc=1, device_id=(outer, mate), device_id_type=MESH)

    for copy in small_copies:
        copy.wait()

    row_list = rows_ref[...]
    sub = lax.broadcasted_iota(jnp.int32, (wide, cmax), 0) + core * half

    def mark(p, carry):
        base = pl.multiple_of(p * wide, wide)
        hot[pl.ds(base, wide), :] = jnp.where(sub == row_list - base, 1.0, 0.0).astype(BF16)
        return carry

    lax.fori_loop(0, pairs, mark, 0, unroll=2)

    pl.semaphore_wait(barrier, len(partners) + has_outer.astype(jnp.int32))
    load_send = pltpu.make_async_remote_copy(
        src_ref=load_hbm.at[:, mate_half],
        dst_ref=load_ref.at[own_rows],
        send_sem=load_sem.at[0],
        recv_sem=load_sem.at[1],
        device_id=(comp, mate),
        device_id_type=MESH,
    )
    load_send.start()

    slot_axis = lax.broadcasted_iota(jnp.int32, (cmax, cmax), 0)
    perm[...] = jnp.where(slot_axis == partner_ref[...], 1.0, 0.0).astype(BF16)

    @pl.when(jnp.logical_not(has_outer))
    def _():
        ext[pl.ds(outside_halo, BAND)] = jnp.zeros((BAND, both_nh, blk), BF16)

    def own_of(value):
        return jnp.where(core == 0, value[:nh], value[nh:])

    def mate_of(value):
        return jnp.where(core == 0, value[nh:], value[:nh])

    def factor_of(start, rows, width):
        index = start + lax.broadcasted_iota(jnp.int32, (rows, width), 0)
        wave = jnp.where(index <= H // 2, index, index - H // 2).astype(F32)
        value = freq_ref[0] * wave * (2.0 / H)
        return value * value

    both_first = (harm - core) * nh
    factor_ref[...] = factor_of(both_first, both_nh, wide)
    slot_index = lax.broadcasted_iota(jnp.int32, (1, cmax), 1)
    slot_scale = jnp.where(slot_index < count_ref[0], normal_ref[...], 0.0)
    both_index = both_first + lax.broadcasted_iota(jnp.int32, (both_nh, cmax), 0)
    weight = jnp.where(both_index == 0, 1.0 / TIME_POINTS, 2.0 / TIME_POINTS)
    spring_ratio = spring_ref[...] / normal_ref[...]

    for copy in diag_copies:
        copy.wait()
    load_copy.wait()
    load_send.wait()
    for copies in block_copies:
        for copy in copies:
            copy.start()
    for copy in table_copies:
        copy.start()
    eye = lax.broadcasted_iota(jnp.int32, (blk, blk), 0) == lax.broadcasted_iota(
        jnp.int32, (blk, blk), 1
    )

    def diagonal(ref, p):
        parts = [
            jnp.sum(jnp.where(eye, ref[2 * p + q, 0].astype(F32), 0.0), axis=0, keepdims=True)
            for q in range(2)
        ]
        return jnp.concatenate(parts, axis=1)

    def put_rounded(p, value):
        rounded = value.astype(BF16)
        for q in range(2):
            ext[BAND + 2 * p + q] = rounded[:, q * blk : (q + 1) * blk]

    def lanes(p):
        return pl.ds(pl.multiple_of(p * wide, wide), wide)

    def start_field(p, gathered):
        stiff_diag = diagonal(stiff_ref, p)
        mass_diag = diagonal(mass_ref, p)
        dynamic = stiff_diag - factor_ref[...] * mass_diag
        inverse = 1.0 / dynamic
        value = load_ref[:, lanes(p)] * inverse
        dyn_ref[p] = dynamic
        inv_ref[p] = inverse
        field[p] = value
        put_rounded(p, value)
        high, low = halves(value)
        diagonals = jnp.concatenate(
            [jnp.broadcast_to(part, (8, wide)) for part in (stiff_diag, mass_diag)], axis=0
        )
        left = jnp.concatenate([high, low, diagonals.astype(BF16)], axis=0)
        return gathered + product(left, hot[lanes(p), :], NN)

    def part_copy(k):
        return pltpu.make_async_remote_copy(
            src_ref=part_ref.at[k, pl.ds(0, nh + 16 if k == 0 else nh)],
            dst_ref=mate_part.at[k, pl.ds(0, nh + 16 if k == 0 else nh)],
            send_sem=part_send.at[k],
            recv_sem=part_recv.at[k],
            device_id=(comp, mate),
            device_id_type=MESH,
        )

    def halo_copies(k):
        out = pltpu.make_async_remote_copy(
            src_ref=ext.at[pl.ds(BAND + outside * BAND, BAND)],
            dst_ref=halo.at[k, 0],
            send_sem=halo_send.at[k, 0],
            recv_sem=halo_recv.at[k, 0],
            device_id=(outer, mate),
            device_id_type=MESH,
        )
        across = pltpu.make_async_remote_copy(
            src_ref=ext.at[pl.ds(BAND + inside * BAND, BAND)],
            dst_ref=halo.at[k, 1],
            send_sem=halo_send.at[k, 1],
            recv_sem=halo_recv.at[k, 1],
            device_id=(comp, mate),
            device_id_type=MESH,
        )
        return out, across

    def start_out(k):
        @pl.when(has_outer)
        def _():
            halo_copies(k)[0].start()

    own = pl.ds(pl.multiple_of(harm * nh, nh), nh)

    def share_copies(k):
        return [
            pltpu.make_async_remote_copy(
                src_ref=shared.at[k, 0, own],
                dst_ref=shared.at[k, 0 if i < harm_size - 1 else 1, own],
                send_sem=share_send.at[k, i],
                recv_sem=share_recv.at[k, i],
                device_id=partner,
                device_id_type=MESH,
            )
            for i, partner in enumerate(partners)
        ]

    def share(k, listed):
        listed_ref[...] = listed
        change = listed if k == 0 else listed - sent_ref[...]
        rounded = change.astype(BF16)
        shared[k, 0, own] = rounded
        for copy in share_copies(k):
            copy.start()
        sent = rounded.astype(F32)
        sent_ref[...] = sent if k == 0 else sent_ref[...] + sent

    def in_order(body, carry, after_outside=None):
        for n, c in enumerate([outside, *middle, inside]):
            carry = lax.fori_loop(0, span, lambda i, now, c=c: body(c * span + i, now), carry, unroll=span)
            if n == 0 and after_outside is not None:
                after_outside()
        return carry

    gathered = in_order(
        start_field, jnp.zeros((2 * both_nh + 16, cmax), F32), lambda: start_out(0)
    )
    listed = folded(gathered[: 2 * both_nh])
    part_ref[0, pl.ds(0, nh)] = mate_of(listed)
    part_ref[0, pl.ds(nh, 16)] = gathered[2 * both_nh :]
    part_copy(0).start()
    halo_copies(0)[1].start()
    listed_ref[...] = own_of(listed)

    def apply_rows(c, gathered):
        def body(i, carry):
            p = c * span + i
            applied = []
            for q in range(2):
                r = 2 * p + q
                picked = jnp.concatenate(
                    [
                        ext[
                            jnp.clip(
                                cols_ref[s, row0 + r] - first_row + BAND, 0, ext.shape[0] - 1
                            )
                        ]
                        for s in range(slots)
                    ],
                    axis=1,
                )
                blocks = jnp.concatenate(
                    [
                        jnp.concatenate([ref[r, s] for s in range(slots)], axis=1)
                        for ref in (stiff_ref, mass_ref)
                    ],
                    axis=0,
                )
                both = product(picked, blocks, NT)
                applied.append(both[:, :blk] - factor_ref[:, :blk] * both[:, blk:])
            rounded = jnp.concatenate([ext[BAND + 2 * p + q] for q in range(2)], axis=1)
            gap = field[p] - rounded.astype(F32)
            value = load_ref[:, lanes(p)] - jnp.concatenate(applied, axis=1) - dyn_ref[p] * gap
            shift[p] = value
            if carry is None:
                return carry
            return carry + product(stacked(value), hot[lanes(p), :], NN)

        return lax.fori_loop(0, span, body, gathered, unroll=span)

    part_copy(0).wait()
    both_parts = part_ref[0, pl.ds(nh, 16)] + mate_part[0, pl.ds(nh, 16)]
    slot_dynamic = both_parts[:1] - factor_of(harm * nh, nh, cmax) * both_parts[8:9]
    slot_inverse[...] = 1.0 / slot_dynamic
    share(0, listed_ref[...] + mate_part[0, pl.ds(0, nh)])

    for k in range(ITERS):
        out, across = halo_copies(k)
        last = k == ITERS - 1

        def take_blocks(n):
            if k == 0:
                for copy in block_copies[n]:
                    copy.wait()

        gathered = None if last else jnp.zeros((2 * both_nh, cmax), F32)
        across.wait()
        ext[pl.ds(inside_halo, BAND)] = halo[k, 1]
        take_blocks(0)
        gathered = apply_rows(inside, gathered)
        for n, c in enumerate(middle):
            take_blocks(1 + n)
            gathered = apply_rows(c, gathered)

        @pl.when(has_outer)
        def _():
            out.wait()
            ext[pl.ds(outside_halo, BAND)] = halo[k, 0]

        take_blocks(chunks - 1)
        gathered = apply_rows(outside, gathered)
        if not last:
            listed = folded(gathered)
            own_part = own_of(listed)
            part_ref[k + 1, pl.ds(0, nh)] = mate_of(listed)
            part_copy(k + 1).start()

        if k == 0:
            for copy in table_copies:
                copy.wait()
        for copy in share_copies(k):
            copy.wait()
        change = shared[k, 0].astype(F32) - product(shared[k, 1], perm[...], NN)
        relative = change if k == 0 else relative_ref[...] + change
        relative_ref[...] = relative
        rel_parts[...] = stacked(relative * spring_ratio)
        total = jnp.zeros((2 * both_nh, cmax), F32)
        step_points = 2 * H
        for t in range(0, TIME_POINTS, step_points):
            values = product(time_ref[pl.ds(t, step_points), :], rel_parts[...], NN)
            wave = jnp.tanh(values).astype(BF16)
            total = total + product(back_ref[:, pl.ds(t, step_points)], wave, NN)
        force = folded(total) * weight * slot_scale
        projected = stacked(force)
        if not last:
            part_copy(k + 1).wait()
            listed = own_part + mate_part[k + 1, pl.ds(0, nh)] - own_of(force)
            share(k + 1, listed_ref[...] + listed * slot_inverse[...])

        def finish(p, carry):
            nonlinear = folded(product(projected, hot[lanes(p), :], NT))
            residual = shift[p] - nonlinear
            value = field[p] + residual * inv_ref[p]
            if last:
                column = pl.ds(pl.multiple_of(core * half + p * wide, wide), wide)
                for n, (target, result) in enumerate(((disp_out, value), (res_out, residual))):
                    target[:, column] = own_of(result)
                    out_stage[n, :, lanes(p)] = mate_of(result)
            else:
                field[p] = value
                put_rounded(p, value)
            return carry

        if last:
            results = []
            for m, c in enumerate(range(chunks)):
                lax.fori_loop(c * span, (c + 1) * span, finish, 0, unroll=span)
                for n, target in enumerate((disp_out, res_out)):
                    width = BAND * blk
                    column = pl.ds(pl.multiple_of(core * half + c * width, width), width)
                    results.append(
                        pltpu.make_async_remote_copy(
                            src_ref=out_stage.at[n, :, pl.ds(c * width, width)],
                            dst_ref=target.at[:, column],
                            send_sem=out_send.at[m, n],
                            recv_sem=out_recv.at[m, n],
                            device_id=(comp, mate),
                            device_id_type=MESH,
                        )
                    )
                    results[-1].start()
            for copy in results:
                copy.wait()
        else:
            in_order(finish, 0, lambda: start_out(k + 1))
            halo_copies(k + 1)[1].start()


def local(comp_size, harm_size, *arrays):
    load, stiff_blocks, mass_blocks, block_cols = arrays[:4]
    nh, dofs = load.shape
    both_nh = 2 * nh
    all_rows, slots, blk, _ = stiff_blocks.shape
    block_rows = all_rows // 2
    held = (block_rows, slots, blk, blk)
    cmax = arrays[4].shape[1]
    to_time, back = host_tables(harm_size // 2)
    vmem = pl.BlockSpec(memory_space=pltpu.VMEM)
    smem = pl.BlockSpec(memory_space=pltpu.SMEM)
    hbm = pl.BlockSpec(memory_space=pltpu.HBM)
    wide = (block_rows // 2, both_nh, 2 * blk)
    dma = pltpu.SemaphoreType.DMA
    places = [hbm, hbm, hbm, hbm, hbm, hbm, smem, hbm, hbm, smem, hbm, hbm]
    operands = (load, stiff_blocks, mass_blocks, block_cols.T, *arrays[4:], jnp.asarray(to_time), jnp.asarray(back))
    return pl.pallas_call(
        functools.partial(kernel, comp_size, harm_size),
        out_shape=(jax.ShapeDtypeStruct((nh, dofs), F32),) * 2,
        in_specs=places,
        out_specs=(vmem, vmem),
        scratch_shapes=[
            pltpu.SMEM((slots, all_rows), jnp.int32),
            pltpu.VMEM((1, cmax), jnp.int32),
            pltpu.VMEM((1, cmax), jnp.int32),
            pltpu.VMEM((1, cmax), F32),
            pltpu.VMEM((1, cmax), F32),
            pltpu.VMEM((both_nh, 2 * blk), F32),
            pltpu.VMEM((both_nh, dofs // 2), F32),
            pltpu.VMEM(to_time.shape, BF16),
            pltpu.VMEM(back.shape[1:], BF16),
            pltpu.VMEM(held, BF16),
            pltpu.VMEM(held, BF16),
            pltpu.VMEM(wide, F32),
            pltpu.VMEM(wide, F32),
            pltpu.VMEM(wide, F32),
            pltpu.VMEM(wide, F32),
            pltpu.VMEM((nh, cmax), F32),
            pltpu.VMEM((dofs // 2, cmax), BF16),
            pltpu.VMEM((cmax, cmax), BF16),
            pltpu.VMEM((block_rows + 2 * BAND, both_nh, blk), BF16),
            pltpu.VMEM((ITERS, 2, BAND, both_nh, blk), BF16),
            pltpu.VMEM((ITERS, nh + 16, cmax), F32),
            pltpu.VMEM((ITERS, nh + 16, cmax), F32),
            pltpu.VMEM((nh, cmax), F32),
            pltpu.VMEM((nh, cmax), F32),
            pltpu.VMEM((ITERS, 2, H, cmax), BF16),
            pltpu.VMEM((H, cmax), F32),
            pltpu.VMEM((2 * H, cmax), BF16),
            pltpu.VMEM((2, nh, dofs // 2), F32),
            dma((5,)),
            dma((3,)),
            dma((2,)),
            dma((block_rows // BAND, 2)),
            dma((2,)),
            dma((ITERS, 2)),
            dma((ITERS, 2)),
            dma((ITERS,)),
            dma((ITERS,)),
            dma((ITERS, 2 * harm_size - 1)),
            dma((ITERS, 2 * harm_size - 1)),
            dma((block_rows // BAND, 2)),
            dma((block_rows // BAND, 2)),
        ],
        compiler_params=pltpu.CompilerParams(
            collective_id=0, has_side_effects=True, vmem_limit_bytes=52 * 1024 * 1024
        ),
    )(
        *(
            pltpu.with_memory_space_constraint(value, pltpu.HBM) if where is hbm else value
            for value, where in zip(operands, places)
        )
    )


def solution(mesh):
    placed = (
        P("harm", "comp"),
        P("comp", None, None, None),
        P("comp", None, None, None),
        P("comp", None),
        P("comp", None),
        P("comp", None),
        P("comp"),
        P("comp", None),
        P("comp", None),
        P(),
    )
    return jax.shard_map(
        functools.partial(local, mesh.shape["comp"], mesh.shape["harm"]),
        mesh=mesh,
        in_specs=placed,
        out_specs=(P("harm", "comp"), P("harm", "comp")),
        check_vma=False,
    )
```

time: 40 us -> 37 us (0.925)
  Pallas kernels: 36.1 us -> 32.7 us
    pallas_call x1, Pallas kernels: 36.1 us -> 32.7 us  [local(): pl.pallas_call(functools.partial(kernel, comp_size, harm_size), out_shape...]
where the time goes in v2:
time: 37 us; the launch traced here: 36.2 us
  Pallas kernels  32.7 us (88%)
  between operations  1.93 us (5%)
  local copies, waits for them, and re-layouts  1.59 us (4%)
    pallas_call x1, Pallas kernels, local(): pl.pallas_call(functools.partial(kernel, comp_size, harm_size), out_shape...  32.7 us
    unnamed x2, local copies, waits for them, and re-layouts  1.59 us

profile of v2, /device:TPU:0, one launch (start us, length us, event | category | flops | bytes accessed | tf_op | source)
XLA Modules:
  0.0 36.2 jit_solution(2817765514160723603)
XLA Ops:
  1.9 32.7 %shard_map.131 = (f32[32,4096]{1,0:T(8,128)S(1)}, f32[32,4096]{1,0:T(8,128)S(1)}) custom-call(f32[32,4096]{1,0:T(8,128)} %load_hbm.1, bf16[32,8,128,128]{3,2,1,0:T(8,128)(2,1)} %stiff_hbm.1, bf16[32,8,128,128]{3,2,1,0:T(8,128)(2,1)} %mass_hbm.1, s32[8,32]{1,0:T(8,128)} %bitcast.1, s32[1,256]{1,0:T(1,128)} %rows_hbm.1, s32[1,256]{1,0:T(1,128)} %partner_hbm.1, ...), custom_call_target="tpu_custom_call" | custom-call | tf_op jit(solution)/shard_map/pallas_call | solution.py:525
  34.7 0.8 %copy.18 = f32[32,4096]{1,0:T(8,128)} copy(f32[32,4096]{1,0:T(8,128)S(1)} %get-tuple-element.4) | data formatting | bytes 1048576
  35.4 0.8 %copy.19 = f32[32,4096]{1,0:T(8,128)} copy(f32[32,4096]{1,0:T(8,128)S(1)} %get-tuple-element.5) | data formatting | bytes 1048576

commit v3 on v2

--- a/solution.py
+++ b/solution.py
@@ -13,6 +13,7 @@
 TIME_POINTS = 1024
 BAND = 8
 ITERS = 3
+PIECES = 4
 MESH = pl.DeviceIdType.MESH
 F32 = jnp.float32
 BF16 = jnp.bfloat16
@@ -64,12 +65,11 @@
     cols_hbm,
     rows_hbm,
     partner_hbm,
-    count_ref,
     normal_hbm,
     spring_hbm,
-    freq_ref,
     time_hbm,
     back_hbm,
+    scalars_ref,
     disp_out,
     res_out,
     cols_ref,
@@ -200,19 +200,6 @@
     def _():
         pl.semaphore_signal(barrier, inc=1, device_id=(outer, mate), device_id_type=MESH)
 
-    for copy in small_copies:
-        copy.wait()
-
-    row_list = rows_ref[...]
-    sub = lax.broadcasted_iota(jnp.int32, (wide, cmax), 0) + core * half
-
-    def mark(p, carry):
-        base = pl.multiple_of(p * wide, wide)
-        hot[pl.ds(base, wide), :] = jnp.where(sub == row_list - base, 1.0, 0.0).astype(BF16)
-        return carry
-
-    lax.fori_loop(0, pairs, mark, 0, unroll=2)
-
     pl.semaphore_wait(barrier, len(partners) + has_outer.astype(jnp.int32))
     load_send = pltpu.make_async_remote_copy(
         src_ref=load_hbm.at[:, mate_half],
@@ -224,6 +211,19 @@
     )
     load_send.start()
 
+    for copy in small_copies:
+        copy.wait()
+
+    row_list = rows_ref[...]
+    sub = lax.broadcasted_iota(jnp.int32, (wide, cmax), 0) + core * half
+
+    def mark(p, carry):
+        base = pl.multiple_of(p * wide, wide)
+        hot[pl.ds(base, wide), :] = jnp.where(sub == row_list - base, 1.0, 0.0).astype(BF16)
+        return carry
+
+    lax.fori_loop(0, pairs, mark, 0, unroll=2)
+
     slot_axis = lax.broadcasted_iota(jnp.int32, (cmax, cmax), 0)
     perm[...] = jnp.where(slot_axis == partner_ref[...], 1.0, 0.0).astype(BF16)
 
@@ -240,26 +240,19 @@
     def factor_of(start, rows, width):
         index = start + lax.broadcasted_iota(jnp.int32, (rows, width), 0)
         wave = jnp.where(index <= H // 2, index, index - H // 2).astype(F32)
-        value = freq_ref[0] * wave * (2.0 / H)
+        value = scalars_ref[:1, :width] * wave * (2.0 / H)
         return value * value
 
     both_first = (harm - core) * nh
     factor_ref[...] = factor_of(both_first, both_nh, wide)
     slot_index = lax.broadcasted_iota(jnp.int32, (1, cmax), 1)
-    slot_scale = jnp.where(slot_index < count_ref[0], normal_ref[...], 0.0)
+    slot_scale = jnp.where(slot_index.astype(F32) < scalars_ref[1:, :cmax], normal_ref[...], 0.0)
     both_index = both_first + lax.broadcasted_iota(jnp.int32, (both_nh, cmax), 0)
     weight = jnp.where(both_index == 0, 1.0 / TIME_POINTS, 2.0 / TIME_POINTS)
     spring_ratio = spring_ref[...] / normal_ref[...]
 
     for copy in diag_copies:
         copy.wait()
-    load_copy.wait()
-    load_send.wait()
-    for copies in block_copies:
-        for copy in copies:
-            copy.start()
-    for copy in table_copies:
-        copy.start()
     eye = lax.broadcasted_iota(jnp.int32, (blk, blk), 0) == lax.broadcasted_iota(
         jnp.int32, (blk, blk), 1
     )
@@ -279,22 +272,22 @@
     def lanes(p):
         return pl.ds(pl.multiple_of(p * wide, wide), wide)
 
-    def start_field(p, gathered):
+    def start_diagonal(p, gathered):
         stiff_diag = diagonal(stiff_ref, p)
         mass_diag = diagonal(mass_ref, p)
         dynamic = stiff_diag - factor_ref[...] * mass_diag
-        inverse = 1.0 / dynamic
-        value = load_ref[:, lanes(p)] * inverse
         dyn_ref[p] = dynamic
-        inv_ref[p] = inverse
-        field[p] = value
-        put_rounded(p, value)
-        high, low = halves(value)
+        inv_ref[p] = 1.0 / dynamic
         diagonals = jnp.concatenate(
             [jnp.broadcast_to(part, (8, wide)) for part in (stiff_diag, mass_diag)], axis=0
         )
-        left = jnp.concatenate([high, low, diagonals.astype(BF16)], axis=0)
-        return gathered + product(left, hot[lanes(p), :], NN)
+        return gathered + product(diagonals.astype(BF16), hot[lanes(p), :], NN)
+
+    def start_field(p, gathered):
+        value = load_ref[:, lanes(p)] * inv_ref[p]
+        field[p] = value
+        put_rounded(p, value)
+        return gathered + product(stacked(value), hot[lanes(p), :], NN)
 
     def part_copy(k):
         return pltpu.make_async_remote_copy(
@@ -306,29 +299,37 @@
             device_id_type=MESH,
         )
 
+    part_rows = BAND // PIECES
+
+    def from_edge(i):
+        return jnp.where(core == 0, i, PIECES - 1 - i) * part_rows
+
     def halo_copies(k):
-        out = pltpu.make_async_remote_copy(
-            src_ref=ext.at[pl.ds(BAND + outside * BAND, BAND)],
-            dst_ref=halo.at[k, 0],
-            send_sem=halo_send.at[k, 0],
-            recv_sem=halo_recv.at[k, 0],
-            device_id=(outer, mate),
-            device_id_type=MESH,
-        )
+        pieces = [
+            pltpu.make_async_remote_copy(
+                src_ref=ext.at[pl.ds(BAND + outside * BAND + from_edge(i), part_rows)],
+                dst_ref=halo.at[k, 0, pl.ds(i * part_rows, part_rows)],
+                send_sem=halo_send.at[k, 1 + i],
+                recv_sem=halo_recv.at[k, 1 + i],
+                device_id=(outer, mate),
+                device_id_type=MESH,
+            )
+            for i in range(PIECES)
+        ]
         across = pltpu.make_async_remote_copy(
             src_ref=ext.at[pl.ds(BAND + inside * BAND, BAND)],
             dst_ref=halo.at[k, 1],
-            send_sem=halo_send.at[k, 1],
-            recv_sem=halo_recv.at[k, 1],
+            send_sem=halo_send.at[k, 0],
+            recv_sem=halo_recv.at[k, 0],
             device_id=(comp, mate),
             device_id_type=MESH,
         )
-        return out, across
-
-    def start_out(k):
+        return pieces, across
+
+    def start_out(k, i):
         @pl.when(has_outer)
         def _():
-            halo_copies(k)[0].start()
+            halo_copies(k)[0][i].start()
 
     own = pl.ds(pl.multiple_of(harm * nh, nh), nh)
 
@@ -355,26 +356,40 @@
         sent = rounded.astype(F32)
         sent_ref[...] = sent if k == 0 else sent_ref[...] + sent
 
-    def in_order(body, carry, after_outside=None):
-        for n, c in enumerate([outside, *middle, inside]):
-            carry = lax.fori_loop(0, span, lambda i, now, c=c: body(c * span + i, now), carry, unroll=span)
-            if n == 0 and after_outside is not None:
-                after_outside()
+    def run(body, first, count, carry):
+        return lax.fori_loop(0, count, lambda i, now: body(first + i, now), carry, unroll=count)
+
+    def in_order(body, carry, k, then=None):
+        for i in range(PIECES):
+            first = outside * span + from_edge(i) // 2
+            carry = run(body, first, part_rows // 2, carry)
+            start_out(k, i)
+        if then is not None:
+            then()
+        for c in [*middle, inside]:
+            carry = run(body, c * span, span, carry)
         return carry
 
-    gathered = in_order(
-        start_field, jnp.zeros((2 * both_nh + 16, cmax), F32), lambda: start_out(0)
+    slot_diagonals = lax.fori_loop(
+        0, pairs, start_diagonal, jnp.zeros((16, cmax), F32), unroll=span
     )
-    listed = folded(gathered[: 2 * both_nh])
+    part_ref[0, pl.ds(nh, 16)] = slot_diagonals
+    load_copy.wait()
+    load_send.wait()
+    for copies in block_copies:
+        for copy in copies:
+            copy.start()
+    for copy in table_copies:
+        copy.start()
+    gathered = in_order(start_field, jnp.zeros((2 * both_nh, cmax), F32), 0)
+    listed = folded(gathered)
     part_ref[0, pl.ds(0, nh)] = mate_of(listed)
-    part_ref[0, pl.ds(nh, 16)] = gathered[2 * both_nh :]
     part_copy(0).start()
     halo_copies(0)[1].start()
     listed_ref[...] = own_of(listed)
 
-    def apply_rows(c, gathered):
-        def body(i, carry):
-            p = c * span + i
+    def apply_rows(first, count, gathered):
+        def body(p, carry):
             applied = []
             for q in range(2):
                 r = 2 * p + q
@@ -406,7 +421,7 @@
                 return carry
             return carry + product(stacked(value), hot[lanes(p), :], NN)
 
-        return lax.fori_loop(0, span, body, gathered, unroll=span)
+        return run(body, first, count, gathered)
 
     part_copy(0).wait()
     both_parts = part_ref[0, pl.ds(nh, 16)] + mate_part[0, pl.ds(nh, 16)]
@@ -415,7 +430,7 @@
     share(0, listed_ref[...] + mate_part[0, pl.ds(0, nh)])
 
     for k in range(ITERS):
-        out, across = halo_copies(k)
+        pieces, across = halo_copies(k)
         last = k == ITERS - 1
 
         def take_blocks(n):
@@ -427,18 +442,23 @@
         across.wait()
         ext[pl.ds(inside_halo, BAND)] = halo[k, 1]
         take_blocks(0)
-        gathered = apply_rows(inside, gathered)
+        gathered = apply_rows(inside * span, span, gathered)
         for n, c in enumerate(middle):
             take_blocks(1 + n)
-            gathered = apply_rows(c, gathered)
-
-        @pl.when(has_outer)
-        def _():
-            out.wait()
-            ext[pl.ds(outside_halo, BAND)] = halo[k, 0]
+            gathered = apply_rows(c * span, span, gathered)
 
         take_blocks(chunks - 1)
-        gathered = apply_rows(outside, gathered)
+        for i, piece in enumerate(pieces):
+            to_edge = from_edge(PIECES - 1 - i)
+
+            @pl.when(has_outer)
+            def _():
+                piece.wait()
+                landed = halo[k, 0, pl.ds(i * part_rows, part_rows)]
+                ext[pl.ds(outside_halo + to_edge, part_rows)] = landed
+
+            gathered = apply_rows(outside * span + to_edge // 2, part_rows // 2, gathered)
+
         if not last:
             listed = folded(gathered)
             own_part = own_of(listed)
@@ -462,11 +482,6 @@
             total = total + product(back_ref[:, pl.ds(t, step_points)], wave, NN)
         force = folded(total) * weight * slot_scale
         projected = stacked(force)
-        if not last:
-            part_copy(k + 1).wait()
-            listed = own_part + mate_part[k + 1, pl.ds(0, nh)] - own_of(force)
-            share(k + 1, listed_ref[...] + listed * slot_inverse[...])
-
         def finish(p, carry):
             nonlinear = folded(product(projected, hot[lanes(p), :], NT))
             residual = shift[p] - nonlinear
@@ -502,8 +517,25 @@
             for copy in results:
                 copy.wait()
         else:
-            in_order(finish, 0, lambda: start_out(k + 1))
+
+            def send_next():
+                part_copy(k + 1).wait()
+                listed = own_part + mate_part[k + 1, pl.ds(0, nh)] - own_of(force)
+                share(k + 1, listed_ref[...] + listed * slot_inverse[...])
+
+            in_order(finish, 0, k + 1, send_next)
             halo_copies(k + 1)[1].start()
+
+
+def deliver(disp_ref, res_ref, disp_hbm, res_hbm, sems):
+    copies = [
+        pltpu.make_async_copy(source, target, sems.at[i])
+        for i, (source, target) in enumerate(((disp_ref, disp_hbm), (res_ref, res_hbm)))
+    ]
+    for copy in copies:
+        copy.start()
+    for copy in copies:
+        copy.wait()
 
 
 def local(comp_size, harm_size, *arrays):
@@ -516,16 +548,18 @@
     cmax = arrays[4].shape[1]
     to_time, back = host_tables(harm_size // 2)
     vmem = pl.BlockSpec(memory_space=pltpu.VMEM)
-    smem = pl.BlockSpec(memory_space=pltpu.SMEM)
     hbm = pl.BlockSpec(memory_space=pltpu.HBM)
     wide = (block_rows // 2, both_nh, 2 * blk)
     dma = pltpu.SemaphoreType.DMA
-    places = [hbm, hbm, hbm, hbm, hbm, hbm, smem, hbm, hbm, smem, hbm, hbm]
-    operands = (load, stiff_blocks, mass_blocks, block_cols.T, *arrays[4:], jnp.asarray(to_time), jnp.asarray(back))
-    return pl.pallas_call(
+    rows, partner, count, normal, spring, freq = arrays[4:]
+    width = max(cmax, 2 * blk)
+    scalars = jnp.concatenate([jnp.broadcast_to(value.astype(F32), (1, width)) for value in (freq, count)], axis=0)
+    operands = (load, stiff_blocks, mass_blocks, block_cols.T, rows, partner, normal, spring)
+    operands += (jnp.asarray(to_time), jnp.asarray(back))
+    results = pl.pallas_call(
         functools.partial(kernel, comp_size, harm_size),
         out_shape=(jax.ShapeDtypeStruct((nh, dofs), F32),) * 2,
-        in_specs=places,
+        in_specs=[hbm] * len(operands) + [vmem],
         out_specs=(vmem, vmem),
         scratch_shapes=[
             pltpu.SMEM((slots, all_rows), jnp.int32),
@@ -561,8 +595,8 @@
             dma((2,)),
             dma((block_rows // BAND, 2)),
             dma((2,)),
-            dma((ITERS, 2)),
-            dma((ITERS, 2)),
+            dma((ITERS, 1 + PIECES)),
+            dma((ITERS, 1 + PIECES)),
             dma((ITERS,)),
             dma((ITERS,)),
             dma((ITERS, 2 * harm_size - 1)),
@@ -574,11 +608,16 @@
             collective_id=0, has_side_effects=True, vmem_limit_bytes=52 * 1024 * 1024
         ),
     )(
-        *(
-            pltpu.with_memory_space_constraint(value, pltpu.HBM) if where is hbm else value
-            for value, where in zip(operands, places)
-        )
+        *(pltpu.with_memory_space_constraint(value, pltpu.HBM) for value in operands), scalars
     )
+    return pl.pallas_call(
+        deliver,
+        out_shape=(jax.ShapeDtypeStruct((nh, dofs), F32),) * 2,
+        in_specs=[vmem, vmem],
+        out_specs=(hbm, hbm),
+        scratch_shapes=[dma((2,))],
+        compiler_params=pltpu.CompilerParams(vmem_limit_bytes=2 * 1024 * 1024),
+    )(*(pltpu.with_memory_space_constraint(value, pltpu.VMEM) for value in results))
 
 
 def solution(mesh):

time: 37 us -> 34.8 us (0.941); the launches traced: 36.2 us -> 34.6 us
  local copies, waits for them, and re-layouts: 1.59 us -> 0.07 us
    unnamed x2 -> x0, local copies, waits for them, and re-layouts: 1.59 us -> none
    pallas_call x1, Pallas kernels: 32.7 us -> 31.6 us  [local(): pl.pallas_call(functools.partial(kernel, comp_size, harm_size), out_shape...]
    pallas_call x0 -> x1, Pallas kernels: none -> 0.99 us  [local(): pl.pallas_call(deliver, out_shape=(jax.ShapeDtypeStruct((nh, dofs), F32),...]
where the time goes in v3:
time: 34.8 us; the launch traced here: 34.6 us
  Pallas kernels  32.6 us (94%)
  between operations  1.94 us (6%)
    pallas_call x1, Pallas kernels, local(): pl.pallas_call(functools.partial(kernel, comp_size, harm_size), out_shape...  31.6 us
    pallas_call x1, Pallas kernels, local(): pl.pallas_call(deliver, out_shape=(jax.ShapeDtypeStruct((nh, dofs), F32),...  0.99 us

profile of v3, /device:TPU:0, one launch (start us, length us, event | category | flops | bytes accessed | tf_op | source)
XLA Modules:
  0.0 34.6 jit_solution(12103281057513530591)
XLA Ops:
  1.9 0.1 concatenate.6.scalars_ref
  2.0 31.6 %shard_map.131 = (f32[32,4096]{1,0:T(8,128)S(1)}, f32[32,4096]{1,0:T(8,128)S(1)}) custom-call(f32[32,4096]{1,0:T(8,128)} %load_hbm.1, bf16[32,8,128,128]{3,2,1,0:T(8,128)(2,1)} %stiff_hbm.1, bf16[32,8,128,128]{3,2,1,0:T(8,128)(2,1)} %mass_hbm.1, s32[8,32]{1,0:T(8,128)} %bitcast.2, s32[1,256]{1,0:T(1,128)} %rows_hbm.1, s32[1,256]{1,0:T(1,128)} %partner_hbm.1, ...), custom_call_target="tpu_custom_call" | custom-call | tf_op jit(solution)/shard_map/pallas_call | solution.py:559
  33.6 1.0 %shard_map.132 = (f32[32,4096]{1,0:T(8,128)}, f32[32,4096]{1,0:T(8,128)}) custom-call(f32[32,4096]{1,0:T(8,128)S(1)} %get-tuple-element.4.disp_ref, f32[32,4096]{1,0:T(8,128)S(1)} %get-tuple-element.5.res_ref), custom_call_target="tpu_custom_call" | custom-call | tf_op jit(solution)/shard_map/pallas_call | solution.py:613
  (1 shorter events, 0.0 us)

commit v4 on v3

--- a/solution.py
+++ b/solution.py
@@ -111,6 +111,8 @@
     part_recv,
     share_send,
     share_recv,
+    forward_send,
+    forward_recv,
     out_send,
     out_recv,
 ):
@@ -333,18 +335,37 @@
 
     own = pl.ds(pl.multiple_of(harm * nh, nh), nh)
 
+    same_core = [lax.rem(harm + 2 * step, harm_size) for step in range(harm_size // 2)]
+    holders = [(0, comp, index) for index in same_core] + [(1, facing, index) for index in same_core]
+
     def share_copies(k):
         return [
             pltpu.make_async_remote_copy(
                 src_ref=shared.at[k, 0, own],
-                dst_ref=shared.at[k, 0 if i < harm_size - 1 else 1, own],
+                dst_ref=shared.at[k, group, own],
                 send_sem=share_send.at[k, i],
                 recv_sem=share_recv.at[k, i],
-                device_id=partner,
+                device_id=(place, index),
                 device_id_type=MESH,
             )
-            for i, partner in enumerate(partners)
+            for i, (group, place, index) in enumerate(holders[1:])
         ]
+
+    def forward_copies(k):
+        copies = []
+        for i, (group, _, index) in enumerate(holders):
+            rows = pl.ds(pl.multiple_of(index * nh, nh), nh)
+            copies.append(
+                pltpu.make_async_remote_copy(
+                    src_ref=shared.at[k, group, rows],
+                    dst_ref=shared.at[k, group, rows],
+                    send_sem=forward_send.at[k, i],
+                    recv_sem=forward_recv.at[k, i],
+                    device_id=(comp, mate),
+                    device_id_type=MESH,
+                )
+            )
+        return copies
 
     def share(k, listed):
         listed_ref[...] = listed
@@ -458,6 +479,11 @@
                 ext[pl.ds(outside_halo + to_edge, part_rows)] = landed
 
             gathered = apply_rows(outside * span + to_edge // 2, part_rows // 2, gathered)
+            if i == 1:
+                for copy in share_copies(k):
+                    copy.wait()
+                for copy in forward_copies(k):
+                    copy.start()
 
         if not last:
             listed = folded(gathered)
@@ -468,7 +494,7 @@
         if k == 0:
             for copy in table_copies:
                 copy.wait()
-        for copy in share_copies(k):
+        for copy in forward_copies(k):
             copy.wait()
         change = shared[k, 0].astype(F32) - product(shared[k, 1], perm[...], NN)
         relative = change if k == 0 else relative_ref[...] + change
@@ -523,7 +549,8 @@
                 listed = own_part + mate_part[k + 1, pl.ds(0, nh)] - own_of(force)
                 share(k + 1, listed_ref[...] + listed * slot_inverse[...])
 
-            in_order(finish, 0, k + 1, send_next)
+            send_next()
+            in_order(finish, 0, k + 1)
             halo_copies(k + 1)[1].start()
 
 
@@ -599,8 +626,10 @@
             dma((ITERS, 1 + PIECES)),
             dma((ITERS,)),
             dma((ITERS,)),
-            dma((ITERS, 2 * harm_size - 1)),
-            dma((ITERS, 2 * harm_size - 1)),
+            dma((ITERS, harm_size - 1)),
+            dma((ITERS, harm_size - 1)),
+            dma((ITERS, harm_size)),
+            dma((ITERS, harm_size)),
             dma((block_rows // BAND, 2)),
             dma((block_rows // BAND, 2)),
         ],

time: 34.8 us -> 32.8 us (0.943)
  Pallas kernels: 32.6 us -> 30.7 us
    pallas_call x1, Pallas kernels: 31.6 us -> 29.7 us  [local(): pl.pallas_call(functools.partial(kernel, comp_size, harm_size), out_shape...]
where the time goes in v4:
time: 32.8 us; the launch traced here: 32.7 us
  Pallas kernels  30.7 us (94%)
  between operations  1.94 us (6%)
    pallas_call x1, Pallas kernels, local(): pl.pallas_call(functools.partial(kernel, comp_size, harm_size), out_shape...  29.7 us
    pallas_call x1, Pallas kernels, local(): pl.pallas_call(deliver, out_shape=(jax.ShapeDtypeStruct((nh, dofs), F32),...  0.99 us

profile of v4, /device:TPU:0, one launch (start us, length us, event | category | flops | bytes accessed | tf_op | source)
XLA Modules:
  0.0 32.7 jit_solution(13172067492330096308)
XLA Ops:
  1.9 0.1 concatenate.6.scalars_ref
  2.0 29.7 %shard_map.131 = (f32[32,4096]{1,0:T(8,128)S(1)}, f32[32,4096]{1,0:T(8,128)S(1)}) custom-call(f32[32,4096]{1,0:T(8,128)} %load_hbm.1, bf16[32,8,128,128]{3,2,1,0:T(8,128)(2,1)} %stiff_hbm.1, bf16[32,8,128,128]{3,2,1,0:T(8,128)(2,1)} %mass_hbm.1, s32[8,32]{1,0:T(8,128)} %bitcast.2, s32[1,256]{1,0:T(1,128)} %rows_hbm.1, s32[1,256]{1,0:T(1,128)} %partner_hbm.1, ...), custom_call_target="tpu_custom_call" | custom-call | tf_op jit(solution)/shard_map/pallas_call | solution.py:586
  31.7 1.0 %shard_map.132 = (f32[32,4096]{1,0:T(8,128)}, f32[32,4096]{1,0:T(8,128)}) custom-call(f32[32,4096]{1,0:T(8,128)S(1)} %get-tuple-element.4.disp_ref, f32[32,4096]{1,0:T(8,128)S(1)} %get-tuple-element.5.res_ref), custom_call_target="tpu_custom_call" | custom-call | tf_op jit(solution)/shard_map/pallas_call | solution.py:642
  (1 shorter events, 0.0 us)
